TPU v7x, 256 devices: a whole 4x4x8 slice. The times are simulated.
256 devices in a mesh: region: 64 (over x, z, core), level: 4 (over y).
Axes of the slice: x: 4, y: 4, z: 8, core: 2. Of those that a mesh axis runs over, the one named last changes fastest.
Arguments:
- ensemble: bfloat16 [4, 256, 262144], P('level', None, 'region'), may hold values from -6 to 6
- obs_anomaly: bfloat16 [4, 65536, 256], P('level', 'region'), may hold values from -6 to 6
- innovation: bfloat16 [4, 65536], P('level', 'region'), may hold values from -18 to 18
- obs_precision: bfloat16 [4, 65536], P('level', 'region'), may hold values from 0.019897461 to 0.29882812
- owner_region: int32 [4, 65536, 1], P('level', 'region'), may hold values from 0 to 63; in each aligned block of 1024 rows (0 to 1023, 1024 to 2047, ..., all dimensions but the last counted through in order) at most 24 rows name the same one
- neighbours: int32 [64, 3], replicated, may hold values from 0 to 63, all different within a row
Outputs:
- analysis: bfloat16 [4, 256, 262144], P('level', None, 'region')
Inputs may be any that keep to these rules, and one draw needn't show every extreme that they name: `owner_region`: among the 1024 observations of one device (aligned blocks), no region is named more than 24 times, a bound that some block reaches. `neighbours`: each row lists 3 different regions; every region is listed by some row.
All inputs are finite; a program needn't handle non-finite values.
Results may differ from a plain program's by a relative error of at most 0.0059.
Values may be sent and summed in bfloat16 or wider, within the bound.
No kernel may reach another device: no remote copies, remote signals or barrier semaphores. Data moves between devices by JAX's collectives and lax.ppermute only.
A program may use at most 64 MiB of HBM per device.

v0:
```python
import math
import jax
import jax.numpy as jnp
from jax import lax
from jax.sharding import PartitionSpec as P

NSTEPS = 4
TAPER = 0.6


def cut_along(value, dim, count):
    before, after = (value.shape[:dim], value.shape[dim + 1 :])
    return jnp.moveaxis(value.reshape(*before, count, -1, *after), dim, 0)


def sum_at_owner(value, axis, dim):
    count = lax.axis_size(axis)
    pieces = lax.all_to_all(cut_along(value, dim, count), axis, 0, 0, tiled=True)
    return jnp.sum(pieces, axis=0)


def neighbour_weights(neighbours):
    region_ids = jnp.arange(neighbours.shape[0], dtype=jnp.int32)
    weights = (region_ids[:, None] == region_ids[None, :]).astype(jnp.float32)
    for listed in range(neighbours.shape[1]):
        hit = (neighbours[:, listed][:, None] == region_ids[None, :]).astype(jnp.float32)
        weights = weights + TAPER ** (listed + 1) * hit
    return weights


def inverse_root(matrix):
    order_size = matrix.shape[0]
    identity = jnp.eye(order_size, dtype=jnp.float32)
    norm_scale = 0.5 * jnp.sqrt(jnp.sum(matrix * matrix))
    root_iter = matrix / norm_scale
    inverse_iter = identity
    for newton_step in range(NSTEPS):
        correction = 1.5 * identity - 0.5 * jnp.dot(
            inverse_iter, root_iter, precision=lax.Precision.HIGHEST
        )
        root_iter = jnp.dot(root_iter, correction, precision=lax.Precision.HIGHEST)
        inverse_iter = jnp.dot(correction, inverse_iter, precision=lax.Precision.HIGHEST)
    return inverse_iter / jnp.sqrt(norm_scale)


def analysis_weights(covariance, innovation_sum):
    order_size = covariance.shape[0]
    identity = jnp.eye(order_size, dtype=jnp.float32)
    precision_matrix = covariance + (order_size - 1.0) * identity
    root = inverse_root(precision_matrix)
    inner = jnp.dot(root, innovation_sum, precision=lax.Precision.HIGHEST)
    mean_shift = jnp.dot(root, inner, precision=lax.Precision.HIGHEST)
    return (math.sqrt(order_size - 1.0) * root + mean_shift[:, None]).astype(jnp.bfloat16)


def update_columns(column_block, transform):
    average = jnp.mean(column_block.astype(jnp.float32), axis=0)
    anomaly = (column_block.astype(jnp.float32) - average[None, :]).astype(jnp.bfloat16)
    combined = lax.dot_general(
        transform, anomaly, (((0,), (0,)), ((), ())), preferred_element_type=jnp.float32
    )
    return (combined + average[None, :]).astype(jnp.bfloat16)


def level_factor(distance, levels):
    factor = jnp.zeros(distance.shape, jnp.float32)
    for apart in range(levels):
        factor = factor + 0.5**apart * (distance == apart).astype(jnp.float32)
    return factor


def body(ensemble, obs_anomaly, innovation, obs_precision, owner_region, neighbours):
    regions = lax.axis_size("region")
    levels = lax.axis_size("level")
    my_level = lax.axis_index("level")
    members = obs_anomaly.shape[2]
    local_obs = obs_anomaly.shape[1]
    capacity = 3 * local_obs // (2 * regions)
    slot_count = (neighbours.shape[1] + 1) * capacity
    region_weight = neighbour_weights(neighbours)
    owner_ids = owner_region[0, :, 0]
    region_ids = jnp.arange(regions, dtype=jnp.int32)
    owner_table = (owner_ids[:, None] == region_ids[None, :]).astype(jnp.float32)
    dest_weight = jnp.dot(owner_table, region_weight.T, precision=lax.Precision.HIGHEST)
    live = dest_weight > 0
    position = jnp.cumsum(live.astype(jnp.int32), axis=0) - 1
    gain = (dest_weight * obs_precision[0].astype(jnp.float32)[:, None]).astype(jnp.bfloat16)
    slot_ids = jnp.arange(slot_count, dtype=jnp.int32)
    placement = jnp.logical_and(
        live.T[:, None, :], position.T[:, None, :] == slot_ids[None, :, None]
    )
    place_float = placement.astype(jnp.float32)
    send_rows = jnp.einsum(
        "rso,om->rsm",
        placement.astype(jnp.bfloat16),
        obs_anomaly[0],
        preferred_element_type=jnp.float32,
    ).astype(jnp.bfloat16)
    send_gain = jnp.einsum(
        "rso,or->rs", place_float, gain.astype(jnp.float32), precision=lax.Precision.HIGHEST
    ).astype(jnp.bfloat16)
    send_innov = jnp.einsum(
        "rso,o->rs", place_float, innovation[0].astype(jnp.float32), precision=lax.Precision.HIGHEST
    ).astype(jnp.bfloat16)
    received = (
        lax.all_to_all(send_rows, "region", split_axis=0, concat_axis=0, tiled=True),
        lax.all_to_all(send_gain, "region", split_axis=0, concat_axis=0, tiled=True),
        lax.all_to_all(send_innov, "region", split_axis=0, concat_axis=0, tiled=True),
    )
    routed_rows = received[0].reshape(-1, members)
    routed_gain = received[1].reshape(-1)
    routed_innov = received[2].reshape(-1)
    weighted = (routed_gain.astype(jnp.float32)[:, None] * routed_rows.astype(jnp.float32)).astype(
        jnp.bfloat16
    )
    own_cov = jnp.dot(weighted.T, routed_rows, preferred_element_type=jnp.float32)
    own_sum = jnp.dot(routed_innov, weighted, preferred_element_type=jnp.float32)
    stacked = jnp.tile(own_cov, (levels, 1))
    target_level = jnp.arange(members * lax.axis_size("level"), dtype=jnp.int32) // members
    factor = level_factor(jnp.abs(target_level - my_level), levels)
    covariance = sum_at_owner(factor[:, None] * stacked, "level", 0)
    level_ids = jnp.arange(levels, dtype=jnp.int32)
    sum_terms = level_factor(jnp.abs(level_ids - my_level), levels)[:, None] * own_sum[None, :]
    all_sums = lax.psum(sum_terms, "level")
    innovation_sum = lax.dynamic_index_in_dim(all_sums, my_level, 0, keepdims=False)
    transform = analysis_weights(covariance, innovation_sum)
    return update_columns(ensemble[0], transform)[None]


def solution(mesh):
    return jax.shard_map(
        body,
        mesh=mesh,
        in_specs=(
            P("level", None, "region"),
            P("level", "region", None),
            P("level", "region"),
            P("level", "region"),
            P("level", "region", None),
            P(),
        ),
        out_specs=P("level", None, "region"),
        check_vma=False,
    )
```

profile of v0, /device:TPU:2, one launch (start us, length us, event | category | flops | bytes accessed | tf_op | source)
XLA Modules:
  0.0 175.8 jit_solution(10290218327440279134)
XLA Ops:
  0.0 0.0 copy-start
  0.0 0.8 slice_bitcast_fusion.2
  0.8 0.7 convert_element_type.111
  1.5 1.2 fusion.32
  2.9 18.0 %reduce-window.6 = s32[64,8,128]{2,1,0:T(8,128)S(1)} reduce-window(s32[64,8,128]{2,1,0:T(8,128)S(1)} %bitcast.82, s32[]{:T(128)} %constant.70.clone.1), window={size=1x1x128 pad=0_0x0_0x127_0}, to_apply=%region_0.0 | reduce-window | flops 8323072 | bytes 524292 | tf_op jit(solution)/shard_map/reduce-window
  20.9 0.1 slice.20
  21.0 0.1 copy.15
  21.2 0.1 copy.16
  21.3 0.1 add_add_fusion
  21.5 4.8 %fusion.5 = f32[64,1,96]{2,1,0:T(1,128)S(1)} fusion(s32[64,1024]{1,0:T(8,128)S(1)} %bitcast.84, pred[64,1024]{1,0:T(8,128)(4,1)S(1)} %get-tuple-element.6, bf16[1024,64,1]{0,1,2:T(8,128)(2,1)S(1)} %fusion.37), kind=kOutput, calls=%fused_computation.4 | convolution fusion | flops 25165824 | bytes 483328 | tf_op jit(solution)/shard_map/rso,or->rs/dot_general | solution.py:99
  26.2 0.6 copy.17
  26.9 12.0 %all-to-all-start = ((bf16[64,1,96]{2,1,0:T(2,128)(2,1)}), bf16[64,1,96]{2,1,0:T(2,128)(2,1)S(1)}, u32[]{:S(2)}, u32[]{:S(2)}) async-start(bf16[64,1,96]{2,1,0:T(2,128)(2,1)} %copy.17), calls=%async_computation | async-start | bytes 65536 | tf_op jit(solution)/shard_map/all_to_all | solution.py:107
  38.9 0.0 copy-done
  38.9 6.9 %fusion.21 = bf16[64,96,256]{2,1,0:T(8,128)(2,1)} fusion(s32[64,1024]{1,0:T(8,128)S(1)} %bitcast.85, pred[64,1024]{1,0:T(8,128)(4,1)S(1)} %get-tuple-element.6, bf16[1,1024,256]{2,1,0:T(8,128)(2,1)S(1)} %copy-done), kind=kOutput, calls=%fused_computation.23 | convolution fusion | flops 3235381248 | bytes 3997696 | tf_op jit(solution)/shard_map/rso,om->rsm/dot_general | solution.py:93
  45.8 0.0 copy-start.2
  45.8 1.7 all-to-all-done
  47.5 9.0 %all-to-all-start.1 = ((bf16[64,96,256]{2,1,0:T(8,128)(2,1)}), bf16[64,96,256]{2,1,0:T(8,128)(2,1)}, u32[]{:S(2)}, u32[]{:S(2)}) async-start(bf16[64,96,256]{2,1,0:T(8,128)(2,1)} %fusion.21), calls=%async_computation.1 | async-start | bytes 6291456 | tf_op jit(solution)/shard_map/all_to_all | solution.py:106
  56.5 0.0 copy-done.2
  56.5 0.0 copy-start.1
  56.5 4.7 %fusion.1 = f32[1,64,96]{2,0,1:T(1,128)S(1)} fusion(s32[64,1024]{1,0:T(8,128)S(1)} %bitcast.86, pred[64,1024]{1,0:T(8,128)(4,1)S(1)} %get-tuple-element.6, bf16[1,1024]{1,0:T(2,128)(2,1)S(1)} %copy-done.2), kind=kOutput, calls=%fused_computation.2 | convolution fusion | flops 25165824 | bytes 354304 | tf_op jit(solution)/shard_map/rso,o->rs/dot_general | solution.py:102
  61.2 0.6 copy.18
  61.8 0.0 copy-done.1
  61.8 0.3 convert_reduce_fusion
  62.2 66.1 %all-to-all-done.1 = bf16[64,96,256]{2,1,0:T(8,128)(2,1)} async-done(((bf16[64,96,256]{2,1,0:T(8,128)(2,1)}), bf16[64,96,256]{2,1,0:T(8,128)(2,1)}, u32[]{:S(2)}, u32[]{:S(2)}) %all-to-all-start.1) | async-done | bytes 3145760 | tf_op jit(solution)/shard_map/all_to_all | solution.py:106
  128.3 7.3 %all-to-all-start.3 = ((bf16[64,1,96]{2,1,0:T(2,128)(2,1)}), bf16[64,1,96]{2,1,0:T(2,128)(2,1)S(1)}, u32[]{:S(2)}, u32[]{:S(2)}) async-start(bf16[64,1,96]{2,1,0:T(2,128)(2,1)} %copy.18), calls=%async_computation.3 | async-start | bytes 65536 | tf_op jit(solution)/shard_map/all_to_all | solution.py:108
  135.6 4.8 %fusion.30 = f32[256,256]{1,0:T(8,128)S(1)} fusion(bf16[64,96,256]{2,1,0:T(8,128)(2,1)} %all-to-all-done.1, f32[64,96]{1,0:T(8,128)S(1)} %bitcast.89), kind=kOutput, calls=%fused_computation.34 | convolution fusion | flops 810024960 | bytes 3432448 | tf_op jit(solution)/shard_map/dot_general | solution.py:116
  140.4 1.2 broadcast_multiply_fusion
  141.6 2.7 %all-to-all-done.3 = bf16[64,1,96]{2,1,0:T(2,128)(2,1)S(1)} async-done(((bf16[64,1,96]{2,1,0:T(2,128)(2,1)}), bf16[64,1,96]{2,1,0:T(2,128)(2,1)S(1)}, u32[]{:S(2)}, u32[]{:S(2)}) %all-to-all-start.3) | async-done | bytes 12320 | tf_op jit(solution)/shard_map/all_to_all | solution.py:108
  144.2 4.5 %all-to-all-start.2 = ((f32[4,256,256]{2,1,0:T(8,128)}), f32[4,256,256]{2,1,0:T(8,128)}, u32[]{:S(2)}, u32[]{:S(2)}) async-start(f32[4,256,256]{2,1,0:T(8,128)} %broadcast_multiply_fusion), calls=%async_computation.2 | async-start | bytes 2097152 | tf_op jit(solution)/shard_map/all_to_all | solution.py:18
  148.7 2.6 %fusion.15 = f32[1,256,1]{1,0,2:T(1,128)S(1)} fusion(bf16[64,96,256]{2,1,0:T(8,128)(2,1)} %all-to-all-done.1, f32[64,96]{1,0:T(8,128)S(1)} %bitcast.90, bf16[64,1,96]{2,1,0:T(2,128)(2,1)S(1)} %all-to-all-done.3), kind=kOutput, calls=%fused_computation.17 | convolution fusion | flops 7864320 | bytes 3183616 | tf_op jit(solution)/shard_map/dot_general | solution.py:117
  151.3 0.1 broadcast_multiply_fusion.2
  151.4 14.7 %psum.7 = f32[4,256]{1,0:T(4,128)S(1)} all-reduce(f32[4,256]{1,0:T(4,128)S(1)} %broadcast_multiply_fusion.2), channel_id=1, replica_groups=mesh['region'=64,'level'=4] {'level'}, use_global_device_ids=true, to_apply=%region_4.5 | all-reduce | flops 1024 | bytes 8192 | tf_op jit(solution)/shard_map/psum | solution.py:124
  166.1 0.0 all-to-all-done.2
  166.1 1.3 reduce_sum.27
  167.4 0.7 multiply_reduce_fusion
  168.8 0.3 fusion.29
  169.2 0.4 fusion.40
  169.6 0.3 fusion.34
  169.9 0.4 fusion.28
  170.2 0.4 fusion.78
  170.6 0.4 fusion.77
  171.0 0.4 fusion.27
  171.4 0.4 fusion.79
  171.8 0.4 fusion.80
  172.2 0.4 fusion.26
  172.6 0.4 convolution_divide_fusion
  173.0 0.3 convolution_bitcast_fusion
  173.2 0.3 fusion.81
  173.6 2.2 %fusion.14 = bf16[1,256,4096]{2,1,0:T(8,128)(2,1)} fusion(bf16[1,256,4096]{2,1,0:T(8,128)(2,1)S(1)} %copy-done.1, f32[4096]{0:T(1024)S(1)} %broadcast_multiply_fusion.1, f32[256,256]{1,0:T(8,128)S(1)} %convolution_divide_fusion, f32[256]{0:T(256)S(1)} %bitcast.93), kind=kOutput, calls=%fused_computation.16 | convolution fusion | flops 542310400 | bytes 4473856 | tf_op jit(solution)/shard_map/dot_general | solution.py:59
  (12 shorter events, 0.3 us)
Async XLA Ops:
  0.0 38.9 %copy-start = (bf16[1,1024,256]{2,1,0:T(8,128)(2,1)S(1)}, bf16[1,1024,256]{2,1,0:T(8,128)(2,1)}, u32[]{:S(2)}) copy-start(bf16[1,1024,256]{2,1,0:T(8,128)(2,1)} %param.7) | copy-start | bytes 1572868
  26.9 20.6 %all-to-all-start = ((bf16[64,1,96]{2,1,0:T(2,128)(2,1)}), bf16[64,1,96]{2,1,0:T(2,128)(2,1)S(1)}, u32[]{:S(2)}, u32[]{:S(2)}) async-start(bf16[64,1,96]{2,1,0:T(2,128)(2,1)} %copy.17), calls=%async_computation | async-start | bytes 65536 | tf_op jit(solution)/shard_map/all_to_all | solution.py:107
  45.8 10.7 %copy-start.2 = (bf16[1,1024]{1,0:T(2,128)(2,1)S(1)}, bf16[1,1024]{1,0:T(2,128)(2,1)}, u32[]{:S(2)}) copy-start(bf16[1,1024]{1,0:T(2,128)(2,1)} %param.8) | copy-start | bytes 6148
  47.5 80.9 %all-to-all-start.1 = ((bf16[64,96,256]{2,1,0:T(8,128)(2,1)}), bf16[64,96,256]{2,1,0:T(8,128)(2,1)}, u32[]{:S(2)}, u32[]{:S(2)}) async-start(bf16[64,96,256]{2,1,0:T(8,128)(2,1)} %fusion.21), calls=%async_computation.1 | async-start | bytes 6291456 | tf_op jit(solution)/shard_map/all_to_all | solution.py:106
  56.5 5.3 %copy-start.1 = (bf16[1,256,4096]{2,1,0:T(8,128)(2,1)S(1)}, bf16[1,256,4096]{2,1,0:T(8,128)(2,1)}, u32[]{:S(2)}) copy-start(bf16[1,256,4096]{2,1,0:T(8,128)(2,1)} %param.6) | copy-start | bytes 6291460
  128.3 15.9 %all-to-all-start.3 = ((bf16[64,1,96]{2,1,0:T(2,128)(2,1)}), bf16[64,1,96]{2,1,0:T(2,128)(2,1)S(1)}, u32[]{:S(2)}, u32[]{:S(2)}) async-start(bf16[64,1,96]{2,1,0:T(2,128)(2,1)} %copy.18), calls=%async_computation.3 | async-start | bytes 65536 | tf_op jit(solution)/shard_map/all_to_all | solution.py:108
  144.2 21.9 %all-to-all-start.2 = ((f32[4,256,256]{2,1,0:T(8,128)}), f32[4,256,256]{2,1,0:T(8,128)}, u32[]{:S(2)}, u32[]{:S(2)}) async-start(f32[4,256,256]{2,1,0:T(8,128)} %broadcast_multiply_fusion), calls=%async_computation.2 | async-start | bytes 2097152 | tf_op jit(solution)/shard_map/all_to_all | solution.py:18
where the time goes:
time: 176 us
  waiting for transfers between devices  70.4 us (40%)
  starting transfers between devices  32.7 us (19%)
  matrix products  31.8 us (18%)
  other arithmetic  22.6 us (13%)
  blocking collectives  14.7 us (8%)
  local copies, waits for them, and re-layouts  2.54 us (1%)
    all_to_all x1, waiting for transfers between devices, body(): lax.all_to_all(send_rows, 'region', split_axis=0, concat_axis=0, tiled=True)  66.1 us
    another operation x2, other arithmetic  18 us
    psum x1, blocking collectives, body(): all_sums = lax.psum(sum_terms, 'level')  14.7 us
    all_to_all x1, starting transfers between devices, body(): lax.all_to_all(send_gain, 'region', split_axis=0, concat_axis=0, tiled=True)  12 us
    all_to_all x1, starting transfers between devices, body(): lax.all_to_all(send_rows, 'region', split_axis=0, concat_axis=0, tiled=True)  8.98 us
    all_to_all x1, starting transfers between devices, body(): lax.all_to_all(send_innov, 'region', split_axis=0, concat_axis=0, tiled=T...  7.27 us
    dot_general x1, matrix products, body(): jnp.einsum('rso,om->rsm', placement.astype(jnp.bfloat16), obs_anomaly[0],...  6.88 us
    dot_general x1, matrix products, body(): jnp.dot(weighted.T, routed_rows, preferred_element_type=jnp.float32)  4.79 us
  transfers between devices with their start and end apart: 4, of which 3 were waited for; matrix products, arithmetic and copies ran while one was open for 12% of the time, Pallas kernels for 0%

commit v1 on v0

--- a/solution.py
+++ b/solution.py
@@ -121,7 +121,11 @@
     covariance = sum_at_owner(factor[:, None] * stacked, "level", 0)
     level_ids = jnp.arange(levels, dtype=jnp.int32)
     sum_terms = level_factor(jnp.abs(level_ids - my_level), levels)[:, None] * own_sum[None, :]
-    all_sums = lax.psum(sum_terms, "level")
+    all_sums = sum_terms
+    for hop in (1, 2):
+        all_sums = all_sums + lax.ppermute(
+            all_sums, "level", [(dev, dev ^ hop) for dev in range(4)]
+        )
     innovation_sum = lax.dynamic_index_in_dim(all_sums, my_level, 0, keepdims=False)
     transform = analysis_weights(covariance, innovation_sum)
     return update_columns(ensemble[0], transform)[None]

time: 176 us -> 176 us (level)
  blocking collectives: 14.7 us -> 0 us
  waiting for transfers between devices: 70.4 us -> 79.5 us
  starting transfers between devices: 32.7 us -> 37.5 us
    psum x1 -> x0, blocking collectives: 14.7 us -> none  [body(): all_sums = lax.psum(sum_terms, 'level')]
    ppermute x0 -> x2, waiting for transfers between devices: none -> 9.03 us  [body(): lax.ppermute(all_sums, 'level', [(dev, dev ^ hop) for dev in range(4)])]
    ppermute x0 -> x2, starting transfers between devices: none -> 4.78 us  [body(): lax.ppermute(all_sums, 'level', [(dev, dev ^ hop) for dev in range(4)])]
  transfers between devices with their start and end apart: 4 -> 6, of which waited for: 3 -> 4; matrix products, arithmetic and copies ran while one was open for 12% -> 16% of each run, Pallas kernels for 0% -> 0%
where the time goes in v1:
time: 176 us; the launch traced here: 175 us
  waiting for transfers between devices  79.5 us (45%)
  starting transfers between devices  37.5 us (21%)
  matrix products  31.8 us (18%)
  other arithmetic  22.7 us (13%)
  local copies, waits for them, and re-layouts  2.55 us (1%)
    all_to_all x1, waiting for transfers between devices, body(): lax.all_to_all(send_rows, 'region', split_axis=0, concat_axis=0, tiled=True)  66.1 us
    another operation x2, other arithmetic  18 us
    all_to_all x1, starting transfers between devices, body(): lax.all_to_all(send_gain, 'region', split_axis=0, concat_axis=0, tiled=True)  12 us
    ppermute x2, waiting for transfers between devices, body(): lax.ppermute(all_sums, 'level', [(dev, dev ^ hop) for dev in range(4)])  9.03 us
    all_to_all x1, starting transfers between devices, body(): lax.all_to_all(send_rows, 'region', split_axis=0, concat_axis=0, tiled=True)  8.95 us
    all_to_all x1, starting transfers between devices, body(): lax.all_to_all(send_innov, 'region', split_axis=0, concat_axis=0, tiled=T...  7.27 us
    dot_general x1, matrix products, body(): jnp.einsum('rso,om->rsm', placement.astype(jnp.bfloat16), obs_anomaly[0],...  6.85 us
    dot_general x1, matrix products, body(): jnp.dot(weighted.T, routed_rows, preferred_element_type=jnp.float32)  4.79 us
  transfers between devices with their start and end apart: 6, of which 4 were waited for; matrix products, arithmetic and copies ran while one was open for 16% of the time, Pallas kernels for 0%

profile of v1, /device:TPU:2, one launch (start us, length us, event | category | flops | bytes accessed | tf_op | source)
XLA Modules:
  0.0 174.9 jit_solution(8196899781956502718)
XLA Ops:
  0.0 0.0 copy-start
  0.0 0.8 slice_bitcast_fusion.2
  0.8 0.7 convert_element_type.111
  1.5 1.2 fusion.32
  2.9 18.0 %reduce-window.6 = s32[64,8,128]{2,1,0:T(8,128)S(1)} reduce-window(s32[64,8,128]{2,1,0:T(8,128)S(1)} %bitcast.82, s32[]{:T(128)} %constant.70.clone.1), window={size=1x1x128 pad=0_0x0_0x127_0}, to_apply=%region_0.0 | reduce-window | flops 8323072 | bytes 524292 | tf_op jit(solution)/shard_map/reduce-window
  20.9 0.1 slice.20
  21.0 0.1 copy.15
  21.2 0.1 copy.16
  21.3 0.1 add_add_fusion
  21.5 4.8 %fusion.5 = f32[64,1,96]{2,1,0:T(1,128)S(1)} fusion(s32[64,1024]{1,0:T(8,128)S(1)} %bitcast.84, pred[64,1024]{1,0:T(8,128)(4,1)S(1)} %get-tuple-element.6, bf16[1024,64,1]{0,1,2:T(8,128)(2,1)S(1)} %fusion.37), kind=kOutput, calls=%fused_computation.4 | convolution fusion | flops 25165824 | bytes 483328 | tf_op jit(solution)/shard_map/rso,or->rs/dot_general | solution.py:99
  26.2 0.6 copy.17
  26.9 12.0 %all-to-all-start = ((bf16[64,1,96]{2,1,0:T(2,128)(2,1)}), bf16[64,1,96]{2,1,0:T(2,128)(2,1)S(1)}, u32[]{:S(2)}, u32[]{:S(2)}) async-start(bf16[64,1,96]{2,1,0:T(2,128)(2,1)} %copy.17), calls=%async_computation | async-start | bytes 65536 | tf_op jit(solution)/shard_map/all_to_all | solution.py:107
  38.9 0.0 copy-done
  38.9 6.8 %fusion.21 = bf16[64,96,256]{2,1,0:T(8,128)(2,1)} fusion(s32[64,1024]{1,0:T(8,128)S(1)} %bitcast.85, pred[64,1024]{1,0:T(8,128)(4,1)S(1)} %get-tuple-element.6, bf16[1,1024,256]{2,1,0:T(8,128)(2,1)S(1)} %copy-done), kind=kOutput, calls=%fused_computation.23 | convolution fusion | flops 3235381248 | bytes 3997696 | tf_op jit(solution)/shard_map/rso,om->rsm/dot_general | solution.py:93
  45.8 0.0 copy-start.2
  45.8 1.7 all-to-all-done
  47.5 8.9 %all-to-all-start.1 = ((bf16[64,96,256]{2,1,0:T(8,128)(2,1)}), bf16[64,96,256]{2,1,0:T(8,128)(2,1)}, u32[]{:S(2)}, u32[]{:S(2)}) async-start(bf16[64,96,256]{2,1,0:T(8,128)(2,1)} %fusion.21), calls=%async_computation.1 | async-start | bytes 6291456 | tf_op jit(solution)/shard_map/all_to_all | solution.py:106
  56.4 0.0 copy-done.2
  56.4 0.0 copy-start.1
  56.4 4.7 %fusion.1 = f32[1,64,96]{2,0,1:T(1,128)S(1)} fusion(s32[64,1024]{1,0:T(8,128)S(1)} %bitcast.86, pred[64,1024]{1,0:T(8,128)(4,1)S(1)} %get-tuple-element.6, bf16[1,1024]{1,0:T(2,128)(2,1)S(1)} %copy-done.2), kind=kOutput, calls=%fused_computation.2 | convolution fusion | flops 25165824 | bytes 354304 | tf_op jit(solution)/shard_map/rso,o->rs/dot_general | solution.py:102
  61.1 0.6 copy.18
  61.8 0.0 copy-done.1
  61.8 0.3 convert_reduce_fusion
  62.2 66.1 %all-to-all-done.1 = bf16[64,96,256]{2,1,0:T(8,128)(2,1)} async-done(((bf16[64,96,256]{2,1,0:T(8,128)(2,1)}), bf16[64,96,256]{2,1,0:T(8,128)(2,1)}, u32[]{:S(2)}, u32[]{:S(2)}) %all-to-all-start.1) | async-done | bytes 3145760 | tf_op jit(solution)/shard_map/all_to_all | solution.py:106
  128.3 7.3 %all-to-all-start.3 = ((bf16[64,1,96]{2,1,0:T(2,128)(2,1)}), bf16[64,1,96]{2,1,0:T(2,128)(2,1)S(1)}, u32[]{:S(2)}, u32[]{:S(2)}) async-start(bf16[64,1,96]{2,1,0:T(2,128)(2,1)} %copy.18), calls=%async_computation.3 | async-start | bytes 65536 | tf_op jit(solution)/shard_map/all_to_all | solution.py:108
  135.6 4.8 %fusion.30 = f32[256,256]{1,0:T(8,128)S(1)} fusion(bf16[64,96,256]{2,1,0:T(8,128)(2,1)} %all-to-all-done.1, f32[64,96]{1,0:T(8,128)S(1)} %bitcast.89), kind=kOutput, calls=%fused_computation.34 | convolution fusion | flops 810024960 | bytes 3432448 | tf_op jit(solution)/shard_map/dot_general | solution.py:116
  140.4 1.2 broadcast_multiply_fusion
  141.5 2.7 %all-to-all-done.3 = bf16[64,1,96]{2,1,0:T(2,128)(2,1)S(1)} async-done(((bf16[64,1,96]{2,1,0:T(2,128)(2,1)}), bf16[64,1,96]{2,1,0:T(2,128)(2,1)S(1)}, u32[]{:S(2)}, u32[]{:S(2)}) %all-to-all-start.3) | async-done | bytes 12320 | tf_op jit(solution)/shard_map/all_to_all | solution.py:108
  144.2 4.5 %all-to-all-start.2 = ((f32[4,256,256]{2,1,0:T(8,128)}), f32[4,256,256]{2,1,0:T(8,128)}, u32[]{:S(2)}, u32[]{:S(2)}) async-start(f32[4,256,256]{2,1,0:T(8,128)} %broadcast_multiply_fusion), calls=%async_computation.2 | async-start | bytes 2097152 | tf_op jit(solution)/shard_map/all_to_all | solution.py:18
  148.6 2.6 %fusion.15 = f32[1,256,1]{1,0,2:T(1,128)S(1)} fusion(bf16[64,96,256]{2,1,0:T(8,128)(2,1)} %all-to-all-done.1, f32[64,96]{1,0:T(8,128)S(1)} %bitcast.90, bf16[64,1,96]{2,1,0:T(2,128)(2,1)S(1)} %all-to-all-done.3), kind=kOutput, calls=%fused_computation.17 | convolution fusion | flops 7864320 | bytes 3183616 | tf_op jit(solution)/shard_map/dot_general | solution.py:117
  151.2 0.1 broadcast_multiply_fusion.2
  151.3 2.0 %collective-permute-start = (f32[4,256]{1,0:T(4,128)S(1)}, f32[4,256]{1,0:T(4,128)S(1)}, u32[]{:S(2)}, u32[]{:S(2)}) collective-permute-start(f32[4,256]{1,0:T(4,128)S(1)} %broadcast_multiply_fusion.2), channel_id=1, source_target_pairs={{0,1},{1,0},{2,3},{3,2},{4,5},{5,4},{6,7},{7,6},{8,9},{9,8},{10,11... | collective-permute-start | bytes 12296 | tf_op jit(solution)/shard_map/ppermute | solution.py:126
  153.4 9.0 %collective-permute-done = f32[4,256]{1,0:T(4,128)S(1)} collective-permute-done((f32[4,256]{1,0:T(4,128)S(1)}, f32[4,256]{1,0:T(4,128)S(1)}, u32[]{:S(2)}, u32[]{:S(2)}) %collective-permute-start) | collective-permute-done | bytes 4128 | tf_op jit(solution)/shard_map/ppermute | solution.py:126
  162.4 0.1 fusion.78
  162.5 2.7 %collective-permute-start.1 = (f32[4,256]{1,0:T(4,128)S(1)}, f32[4,256]{1,0:T(4,128)S(1)}, u32[]{:S(2)}, u32[]{:S(2)}) collective-permute-start(f32[4,256]{1,0:T(4,128)S(1)} %fusion.78), channel_id=1, source_target_pairs={{0,2},{1,3},{2,0},{3,1},{4,6},{5,7},{6,4},{7,5},{8,10},{9,11},{10,... | collective-permute-start | bytes 12296 | tf_op jit(solution)/shard_map/ppermute | solution.py:126
  165.2 0.0 all-to-all-done.2
  165.2 1.3 reduce_sum.27
  166.5 0.7 multiply_reduce_fusion
  167.9 0.3 fusion.29
  168.3 0.4 fusion.40
  168.7 0.3 fusion.34
  169.0 0.4 fusion.28
  169.3 0.4 fusion.80
  169.7 0.4 fusion.79
  170.1 0.4 fusion.27
  170.5 0.4 fusion.81
  170.9 0.4 fusion.82
  171.3 0.4 fusion.26
  171.7 0.4 convolution_divide_fusion
  172.1 0.0 collective-permute-done.1
  172.1 0.3 convolution_bitcast_fusion
  172.3 0.3 fusion.83
  172.7 2.2 %fusion.14 = bf16[1,256,4096]{2,1,0:T(8,128)(2,1)} fusion(bf16[1,256,4096]{2,1,0:T(8,128)(2,1)S(1)} %copy-done.1, f32[4096]{0:T(1024)S(1)} %broadcast_multiply_fusion.1, f32[256,256]{1,0:T(8,128)S(1)} %convolution_divide_fusion, f32[256]{0:T(256)S(1)} %bitcast.93), kind=kOutput, calls=%fused_computation.16 | convolution fusion | flops 542310400 | bytes 4473856 | tf_op jit(solution)/shard_map/dot_general | solution.py:59
  (12 shorter events, 0.3 us)
Async XLA Ops:
  0.0 38.9 %copy-start = (bf16[1,1024,256]{2,1,0:T(8,128)(2,1)S(1)}, bf16[1,1024,256]{2,1,0:T(8,128)(2,1)}, u32[]{:S(2)}) copy-start(bf16[1,1024,256]{2,1,0:T(8,128)(2,1)} %param.7) | copy-start | bytes 1572868
  26.9 20.6 %all-to-all-start = ((bf16[64,1,96]{2,1,0:T(2,128)(2,1)}), bf16[64,1,96]{2,1,0:T(2,128)(2,1)S(1)}, u32[]{:S(2)}, u32[]{:S(2)}) async-start(bf16[64,1,96]{2,1,0:T(2,128)(2,1)} %copy.17), calls=%async_computation | async-start | bytes 65536 | tf_op jit(solution)/shard_map/all_to_all | solution.py:107
  45.8 10.7 %copy-start.2 = (bf16[1,1024]{1,0:T(2,128)(2,1)S(1)}, bf16[1,1024]{1,0:T(2,128)(2,1)}, u32[]{:S(2)}) copy-start(bf16[1,1024]{1,0:T(2,128)(2,1)} %param.8) | copy-start | bytes 6148
  47.5 80.8 %all-to-all-start.1 = ((bf16[64,96,256]{2,1,0:T(8,128)(2,1)}), bf16[64,96,256]{2,1,0:T(8,128)(2,1)}, u32[]{:S(2)}, u32[]{:S(2)}) async-start(bf16[64,96,256]{2,1,0:T(8,128)(2,1)} %fusion.21), calls=%async_computation.1 | async-start | bytes 6291456 | tf_op jit(solution)/shard_map/all_to_all | solution.py:106
  56.4 5.4 %copy-start.1 = (bf16[1,256,4096]{2,1,0:T(8,128)(2,1)S(1)}, bf16[1,256,4096]{2,1,0:T(8,128)(2,1)}, u32[]{:S(2)}) copy-start(bf16[1,256,4096]{2,1,0:T(8,128)(2,1)} %param.6) | copy-start | bytes 6291460
  128.3 15.9 %all-to-all-start.3 = ((bf16[64,1,96]{2,1,0:T(2,128)(2,1)}), bf16[64,1,96]{2,1,0:T(2,128)(2,1)S(1)}, u32[]{:S(2)}, u32[]{:S(2)}) async-start(bf16[64,1,96]{2,1,0:T(2,128)(2,1)} %copy.18), calls=%async_computation.3 | async-start | bytes 65536 | tf_op jit(solution)/shard_map/all_to_all | solution.py:108
  144.2 21.0 %all-to-all-start.2 = ((f32[4,256,256]{2,1,0:T(8,128)}), f32[4,256,256]{2,1,0:T(8,128)}, u32[]{:S(2)}, u32[]{:S(2)}) async-start(f32[4,256,256]{2,1,0:T(8,128)} %broadcast_multiply_fusion), calls=%async_computation.2 | async-start | bytes 2097152 | tf_op jit(solution)/shard_map/all_to_all | solution.py:18
  151.3 11.1 %collective-permute-start = (f32[4,256]{1,0:T(4,128)S(1)}, f32[4,256]{1,0:T(4,128)S(1)}, u32[]{:S(2)}, u32[]{:S(2)}) collective-permute-start(f32[4,256]{1,0:T(4,128)S(1)} %broadcast_multiply_fusion.2), channel_id=1, source_target_pairs={{0,1},{1,0},{2,3},{3,2},{4,5},{5,4},{6,7},{7,6},{8,9},{9,8},{10,11... | collective-permute-start | bytes 12296 | tf_op jit(solution)/shard_map/ppermute | solution.py:126
  162.5 9.6 %collective-permute-start.1 = (f32[4,256]{1,0:T(4,128)S(1)}, f32[4,256]{1,0:T(4,128)S(1)}, u32[]{:S(2)}, u32[]{:S(2)}) collective-permute-start(f32[4,256]{1,0:T(4,128)S(1)} %fusion.78), channel_id=1, source_target_pairs={{0,2},{1,3},{2,0},{3,1},{4,6},{5,7},{6,4},{7,5},{8,10},{9,11},{10,... | collective-permute-start | bytes 12296 | tf_op jit(solution)/shard_map/ppermute | solution.py:126
